TPU v7x, 512 devices: a whole 4x4x16 slice. The times are simulated.
512 devices in a mesh: wide: 64 (over z, y_hi, core), narrow: 8 (over x, y_lo).
Axes of the slice: x: 4, y: 4 (y_hi: 2, y_lo: 2; y = y_hi * 2 + y_lo), z: 16, core: 2. Of those that a mesh axis runs over, the one named last changes fastest.
Arguments:
- tokens: bfloat16 [512, 8192], P('wide', 'narrow'), may hold values from -6 to 6
- cotangent: bfloat16 [512, 8192], P('wide', 'narrow'), may hold values from -2.390625 to 2.390625
- gate_vals: bfloat16 [8, 64, 12, 128, 128], P('narrow', 'wide'), may hold values from -0.125 to 0.125
- up_vals: bfloat16 [8, 64, 12, 128, 128], P('narrow', 'wide'), may hold values from -0.125 to 0.125
- gu_index: int32 [8, 64, 12], P('narrow', 'wide'), may hold values from 0 to 15, as said below
- gu_count: int32 [8, 64], P('narrow', 'wide'), may hold values from 1 to 12, as said below
- down_vals: bfloat16 [64, 8, 12, 128, 128], P('wide', 'narrow'), may hold values from -0.09375 to 0.09375
- down_index: int32 [64, 8, 12], P('wide', 'narrow'), may hold values from 0 to 15, as said below
- down_count: int32 [64, 8], P('wide', 'narrow'), may hold values from 1 to 12, as said below
Outputs:
- d_tokens: bfloat16 [512, 8192], P('wide', 'narrow')
- gate_grad: bfloat16 [8, 64, 12, 128, 128], P('narrow', 'wide')
- up_grad: bfloat16 [8, 64, 12, 128, 128], P('narrow', 'wide')
- down_grad: bfloat16 [64, 8, 12, 128, 128], P('wide', 'narrow')
Inputs may be any that keep to these rules, and one draw needn't show every extreme that they name: `gu_index`: within each tile all 12 entries are different. `gu_count`: some tile has exactly 12 live slots. `down_index`: within each tile all 12 entries are different. `down_count`: some tile has exactly 12 live slots.
All inputs are finite; a program needn't handle non-finite values.
Results may differ from a plain program's by a relative error of at most 0.005.
Values may be sent and summed in bfloat16 or wider, within the bound.
A program may use at most 64 MiB of HBM per device.

v0:
```python
import jax
import jax.numpy as jnp
from jax import lax
from jax.sharding import PartitionSpec as P

FF = 16384


def apply_blocks(inputs, tile_values, source_blocks, target_blocks, target_total, form):
    block_size = tile_values.shape[-1]
    row_total = inputs.shape[0]
    pieces = inputs.reshape(row_total, inputs.shape[1] // block_size, block_size)
    picked = jnp.take(pieces, source_blocks, axis=1)
    products = jnp.einsum(form, picked, tile_values, preferred_element_type=jnp.float32)
    placer = (target_blocks[:, None] == jnp.arange(target_total, dtype=jnp.int32)[None, :]).astype(
        jnp.float32
    )
    placed = jnp.einsum("rsn,sc->rcn", products, placer, precision=lax.Precision.HIGHEST)
    return placed.reshape(row_total, target_total * block_size)


def block_grads(left, right, left_blocks, right_blocks, alive, block_size):
    row_total = left.shape[0]
    left_parts = jnp.take(
        left.reshape(row_total, left.shape[1] // block_size, block_size), left_blocks, axis=1
    )
    right_parts = jnp.take(
        right.reshape(row_total, right.shape[1] // block_size, block_size), right_blocks, axis=1
    )
    result = jnp.einsum("rsk,rsn->skn", left_parts, right_parts, preferred_element_type=jnp.float32)
    return jnp.where(alive[:, None, None], result, 0.0).astype(jnp.bfloat16)


def on_device(
    tokens, cotangent, gate_vals, up_vals, gu_index, gu_count, down_vals, down_index, down_count
):
    block_size = gate_vals.shape[-1]
    slots_total = gate_vals.shape[2]
    wide_size = lax.axis_size("wide")
    d_blocks = tokens.shape[1] // block_size
    f_blocks = FF // (block_size * wide_size)
    f_width = f_blocks * block_size
    slot_range = jnp.arange(slots_total, dtype=jnp.int32)
    gate_alive = slot_range < gu_count[0, 0]
    down_alive = slot_range < down_count[0, 0]
    gate_rows = gu_index[0, 0] // f_blocks
    gate_cols = gu_index[0, 0] % f_blocks
    down_rows = down_index[0, 0] // d_blocks
    down_cols = down_index[0, 0] % d_blocks
    gate_tile = jnp.where(gate_alive[:, None, None], gate_vals[0, 0], 0)
    up_tile = jnp.where(gate_alive[:, None, None], up_vals[0, 0], 0)
    down_tile = jnp.where(down_alive[:, None, None], down_vals[0, 0], 0)
    paired = jnp.concatenate([gate_tile, up_tile], axis=0)
    paired_rows = jnp.concatenate([gate_rows, gate_rows], axis=0)
    paired_cols = jnp.concatenate([gate_cols, gate_cols + f_blocks], axis=0)
    paired_alive = jnp.concatenate([gate_alive, gate_alive], axis=0)
    x_all = lax.all_gather(tokens, "wide", axis=0, tiled=True)
    dy_all = lax.all_gather(cotangent, "wide", axis=0, tiled=True)
    merged = lax.psum_scatter(
        apply_blocks(x_all, paired, paired_rows, paired_cols, 2 * f_blocks, "rsk,skn->rsn"),
        "narrow",
        scatter_dimension=0,
        tiled=True,
    )
    d_hidden = lax.psum_scatter(
        apply_blocks(dy_all, down_tile, down_cols, down_rows, f_blocks, "rsn,skn->rsk"),
        "narrow",
        scatter_dimension=0,
        tiled=True,
    )
    gate_out = merged[:, :f_width]
    up_out = merged[:, f_width:]
    sigmoid_g = jax.nn.sigmoid(gate_out)
    hidden = (gate_out * sigmoid_g * up_out).astype(jnp.bfloat16)
    d_gate = (d_hidden * up_out * sigmoid_g * (1.0 + gate_out * (1.0 - sigmoid_g))).astype(
        jnp.bfloat16
    )
    d_up = (d_hidden * gate_out * sigmoid_g).astype(jnp.bfloat16)
    hidden_all, dgate_all, dup_all = (
        lax.all_gather(hidden, "narrow", axis=0, tiled=True),
        lax.all_gather(d_gate, "narrow", axis=0, tiled=True),
        lax.all_gather(d_up, "narrow", axis=0, tiled=True),
    )
    down_grad = block_grads(hidden_all, dy_all, down_rows, down_cols, down_alive, block_size)
    grads_pair = jnp.concatenate([dgate_all, dup_all], axis=1)
    both_grads = block_grads(x_all, grads_pair, paired_rows, paired_cols, paired_alive, block_size)
    gate_grad = both_grads[:slots_total]
    up_grad = both_grads[slots_total:]
    d_tokens = lax.psum_scatter(
        apply_blocks(grads_pair, paired, paired_cols, paired_rows, d_blocks, "rsn,skn->rsk"),
        "wide",
        scatter_dimension=0,
        tiled=True,
    ).astype(jnp.bfloat16)
    return (d_tokens, gate_grad[None, None], up_grad[None, None], down_grad[None, None])


def solution(mesh):
    in_specs = (
        P("wide", "narrow"),
        P("wide", "narrow"),
        P("narrow", "wide", None, None, None),
        P("narrow", "wide", None, None, None),
        P("narrow", "wide", None),
        P("narrow", "wide"),
        P("wide", "narrow", None, None, None),
        P("wide", "narrow", None),
        P("wide", "narrow"),
    )
    out_specs = (
        P("wide", "narrow"),
        P("narrow", "wide", None, None, None),
        P("narrow", "wide", None, None, None),
        P("wide", "narrow", None, None, None),
    )
    return jax.shard_map(
        on_device, mesh=mesh, in_specs=in_specs, out_specs=out_specs, check_vma=False
    )
```

profile of v0, /device:TPU:2, one launch (start us, length us, event | category | flops | bytes accessed | tf_op | source)
XLA Modules:
  0.0 692.6 jit_solution(14160900754381156844)
XLA Ops:
  7.2 0.0 all-gather.3.cloned.1.call-start
  7.2 0.7 all-gather.3.cloned.1.call-update
  7.9 0.0 all-gather.5.cloned.1.call-start
  7.9 0.7 all-gather.5.cloned.1.call-update
  8.6 0.0 reduce-scatter.10.cloned.1.call-start
  10.0 1.2 copy.61
  11.2 1.2 copy.62
  12.4 1.9 copy.63
  14.4 1.2 compare_and_fusion.3
  15.5 1.2 broadcast_add_fusion
  16.8 0.9 bitcast_select_fusion.3
  17.7 139.1 %all-gather.3.cloned.1.call-done = bf16[512,1024]{1,0:T(8,128)(2,1)} async-done(((bf16[8,1024]{1,0:T(8,128)(2,1)}), bf16[512,1024]{1,0:T(8,128)(2,1)}) %all-gather.3.cloned.1.call-update) | async-done | bytes 1048592 | tf_op jit(solution)/shard_map/all_gather | solution.py:58
  156.8 1.5 copy.64
  158.3 0.7 copy.65
  159.0 1.9 gather_fusion.1
  160.9 0.0 copy-done.5
  160.9 2.3 convolution_bitcast_fusion
  163.2 3.5 copy.67
  166.8 3.8 convolution_bitcast_fusion.2
  170.5 0.2 copy.93
  170.7 1.0 copy.95
  171.7 0.0 reduce-scatter.10.cloned.1.call-update
  171.8 0.0 reduce-scatter.12.cloned.1.call-start
  171.8 0.0 copy-done.2
  171.8 0.1 compare_and_fusion
  171.9 124.8 %all-gather.5.cloned.1.call-done = bf16[512,1024]{1,0:T(8,128)(2,1)} async-done(((bf16[8,1024]{1,0:T(8,128)(2,1)}), bf16[512,1024]{1,0:T(8,128)(2,1)}) %all-gather.5.cloned.1.call-update) | async-done | bytes 1048592 | tf_op jit(solution)/shard_map/all_gather | solution.py:57
  296.7 1.5 copy.69
  298.2 0.7 copy.70
  298.9 0.0 copy-start.1
  298.9 2.7 gather_fusion.2
  301.6 5.6 fusion.7
  307.2 6.6 copy.71
  313.8 5.1 convolution_bitcast_fusion.1
  318.9 0.4 copy.94
  319.3 1.3 copy.97
  320.6 0.0 reduce-scatter.12.cloned.1.call-update
  320.6 0.0 reduce-scatter.8.cloned.1.call-start
  320.7 0.1 pad_add_fusion.1
  320.8 18.1 %reduce-scatter.10.cloned.1.call-done = f32[64,256]{1,0:T(8,128)} async-done(((f32[512,256]{1,0:T(8,128)}), f32[64,256]{1,0:T(8,128)}) %reduce-scatter.10.cloned.1.call-update) | async-done | bytes 65552 | tf_op jit(solution)/shard_map/reduce_scatter | solution.py:65
  338.8 48.9 %reduce-scatter.12.cloned.1.call-done = f32[64,512]{1,0:T(8,128)} async-done(((f32[512,512]{1,0:T(8,128)}), f32[64,512]{1,0:T(8,128)}) %reduce-scatter.12.cloned.1.call-update) | async-done | bytes 131088 | tf_op jit(solution)/shard_map/reduce_scatter | solution.py:59
  387.8 0.9 multiply_convert_fusion.2
  388.7 28.5 %all_gather.17 = bf16[512,256]{1,0:T(8,128)(2,1)S(1)} all-gather(bf16[64,256]{1,0:T(8,128)(2,1)S(1)} %get-tuple-element.31), channel_id=1, replica_groups=mesh['wide'=64,'narrow'=8] {'narrow'}, dimensions={0}, use_global_device_ids=true | all-gather | bytes 294912 | tf_op jit(solution)/shard_map/all_gather | solution.py:81
  417.2 0.1 copy.77
  417.3 28.5 %all_gather.18 = bf16[512,256]{1,0:T(8,128)(2,1)S(1)} all-gather(bf16[64,256]{1,0:T(8,128)(2,1)S(1)} %get-tuple-element.32), channel_id=1, replica_groups=mesh['wide'=64,'narrow'=8] {'narrow'}, dimensions={0}, use_global_device_ids=true | all-gather | bytes 294912 | tf_op jit(solution)/shard_map/all_gather | solution.py:82
  445.8 0.1 copy.78
  446.0 0.3 copy.79
  446.3 2.7 gather_fusion.3
  449.0 5.7 fusion.10
  454.6 6.6 copy.81
  461.2 4.3 fusion.42
  465.5 0.0 copy-start.7
  465.5 1.8 copy.101
  467.3 0.0 reduce-scatter.8.cloned.1.call-update
  467.4 0.6 pad_add_fusion
  468.0 28.4 %all_gather.19 = bf16[512,256]{1,0:T(8,128)(2,1)S(1)} all-gather(bf16[64,256]{1,0:T(8,128)(2,1)S(1)} %get-tuple-element.33), channel_id=1, replica_groups=mesh['wide'=64,'narrow'=8] {'narrow'}, dimensions={0}, use_global_device_ids=true | all-gather | bytes 294912 | tf_op jit(solution)/shard_map/all_gather | solution.py:80
  496.4 0.1 copy.83
  496.5 0.2 copy.84
  496.7 1.9 gather_fusion
  498.6 2.8 fusion.33
  501.5 0.9 copy.87
  502.4 3.2 select_convert_fusion
  505.7 1.0 slice_bitcast_fusion
  506.6 178.1 %reduce-scatter.8.cloned.1.call-done = f32[8,1024]{1,0:T(8,128)} async-done(((f32[512,1024]{1,0:T(8,128)}), f32[8,1024]{1,0:T(8,128)}) %reduce-scatter.8.cloned.1.call-update) | async-done | bytes 32784 | tf_op jit(solution)/shard_map/reduce_scatter | solution.py:89
  684.8 1.4 convert_element_type.27
  (20 shorter events, 0.1 us)
Async XLA Ops:
  7.2 149.6 %all-gather.3.cloned.1.call-start = ((), (), s32[]{:S(2)}) async-start(), calls=%async_computation.3 | async-start | bytes 1064960 | tf_op jit(solution)/shard_map/all_gather | solution.py:58
  7.9 288.8 %all-gather.5.cloned.1.call-start = ((), (), s32[]{:S(2)}) async-start(), calls=%async_computation.4 | async-start | bytes 1064960 | tf_op jit(solution)/shard_map/all_gather | solution.py:57
  8.6 330.2 %reduce-scatter.10.cloned.1.call-start = ((), (), s32[]{:S(2)}) async-start(), calls=%async_computation.6 | async-start | bytes 589824 | tf_op jit(solution)/shard_map/reduce_scatter | solution.py:65
  14.4 146.5 %copy-start.5 = (pred[12]{0:T(512)(128)(4,1)}, pred[12]{0:T(512)(128)(4,1)S(1)}, u32[]{:S(2)}) copy-start(pred[12]{0:T(512)(128)(4,1)S(1)} %iota_compare_fusion.3) | copy-start | bytes 40
  166.8 5.1 copy-start.2
  166.8 5.1 copy-start.3
  166.8 5.1 copy-start.4
  171.8 216.0 %reduce-scatter.12.cloned.1.call-start = ((), (), s32[]{:S(2)}) async-start(), calls=%async_computation.7 | async-start | bytes 1179648 | tf_op jit(solution)/shard_map/reduce_scatter | solution.py:59
  298.9 2.7 copy-start.1
  320.6 364.1 %reduce-scatter.8.cloned.1.call-start = ((), (), s32[]{:S(2)}) async-start(), calls=%async_computation.5 | async-start | bytes 2129920 | tf_op jit(solution)/shard_map/reduce_scatter | solution.py:89
  465.5 1.9 copy-start.6
  465.5 2.4 copy-start.7
  498.6 3.8 copy-start
Sparse Core Ops, SparseCore 0:
  11.3 145.4 all-gather.2
  160.1 136.5 all-gather.4
  299.5 39.2 reduce-scatter.9
  341.5 46.1 reduce-scatter.11
  467.5 217.2 reduce-scatter.7
where the time goes:
time: 693 us
  waiting for transfers between devices  510 us (74%)
  blocking collectives  85.3 us (12%)
  local copies, waits for them, and re-layouts  42.1 us (6%)
  matrix products  32.8 us (5%)
  between operations  15.3 us (2%)
    reduce_scatter x1, waiting for transfers between devices, on_device(): lax.psum_scatter(apply_blocks(grads_pair, paired, paired_cols, paired_row...  178 us
    all_gather x1, waiting for transfers between devices, on_device(): dy_all = lax.all_gather(cotangent, 'wide', axis=0, tiled=True)  139 us
    all_gather x1, waiting for transfers between devices, on_device(): x_all = lax.all_gather(tokens, 'wide', axis=0, tiled=True)  125 us
    reduce_scatter x1, waiting for transfers between devices, on_device(): lax.psum_scatter(apply_blocks(x_all, paired, paired_rows, paired_cols, 2...  48.9 us
    all_gather x1, blocking collectives, on_device(): lax.all_gather(d_gate, 'narrow', axis=0, tiled=True)  28.5 us
    all_gather x1, blocking collectives, on_device(): lax.all_gather(d_up, 'narrow', axis=0, tiled=True)  28.5 us
    all_gather x1, blocking collectives, on_device(): lax.all_gather(hidden, 'narrow', axis=0, tiled=True)  28.4 us
    reduce_scatter x1, waiting for transfers between devices, on_device(): lax.psum_scatter(apply_blocks(dy_all, down_tile, down_cols, down_rows, f_...  18.1 us
  transfers between devices with their start and end apart: 5, of which 5 were waited for; matrix products, arithmetic and copies ran while one was open for 8% of the time, Pallas kernels for 0%

commit v1 on v0

--- a/solution.py
+++ b/solution.py
@@ -54,7 +54,9 @@
     paired_rows = jnp.concatenate([gate_rows, gate_rows], axis=0)
     paired_cols = jnp.concatenate([gate_cols, gate_cols + f_blocks], axis=0)
     paired_alive = jnp.concatenate([gate_alive, gate_alive], axis=0)
-    x_all = lax.all_gather(tokens, "wide", axis=0, tiled=True)
+    x_all = jnp.concatenate(
+        lax.all_to_all(jnp.stack([tokens] * lax.axis_size("wide")), "wide", 0, 0), axis=0
+    )
     dy_all = lax.all_gather(cotangent, "wide", axis=0, tiled=True)
     merged = lax.psum_scatter(
         apply_blocks(x_all, paired, paired_rows, paired_cols, 2 * f_blocks, "rsk,skn->rsn"),

time: 693 us -> 584 us (0.84)
  the two profiles are of different devices: /device:TPU:2 before, /device:TPU:4 now
where the time goes in v1:
time: 584 us; the launch traced here: 583 us
  waiting for transfers between devices  386 us (66%)
  blocking collectives  84.8 us (15%)
  local copies, waits for them, and re-layouts  40.5 us (7%)
  matrix products  32.8 us (6%)
  starting transfers between devices  19.2 us (3%)
  between operations  15.4 us (3%)
    reduce_scatter x1, waiting for transfers between devices, on_device(): lax.psum_scatter(apply_blocks(grads_pair, paired, paired_cols, paired_row...  179 us
    all_gather x1, waiting for transfers between devices, on_device(): dy_all = lax.all_gather(cotangent, 'wide', axis=0, tiled=True)  141 us
    reduce_scatter x1, waiting for transfers between devices, on_device(): lax.psum_scatter(apply_blocks(x_all, paired, paired_rows, paired_cols, 2...  49.8 us
    all_gather x1, blocking collectives, on_device(): lax.all_gather(d_up, 'narrow', axis=0, tiled=True)  28.6 us
    all_gather x1, blocking collectives, on_device(): lax.all_gather(hidden, 'narrow', axis=0, tiled=True)  28.4 us
    all_gather x1, blocking collectives, on_device(): lax.all_gather(d_gate, 'narrow', axis=0, tiled=True)  27.8 us
    all_to_all x1, starting transfers between devices, on_device(): lax.all_to_all(jnp.stack([tokens] * lax.axis_size('wide')), 'wide', 0, 0)  19 us
    transpose x3, local copies, waits for them, and re-layouts, apply_blocks(): jnp.einsum(form, picked, tile_values, preferred_element_type=jnp.float32)  16.7 us
  transfers between devices with their start and end apart: 5, of which 4 were waited for; matrix products, arithmetic and copies ran while one was open for 9% of the time, Pallas kernels for 0%

profile of v1, /device:TPU:4, one launch (start us, length us, event | category | flops | bytes accessed | tf_op | source)
XLA Modules:
  0.0 583.5 jit_solution(12646750919811987706)
XLA Ops:
  7.2 0.0 copy-start.10
  7.2 1.9 stack.2
  9.1 19.0 %all-to-all-start = ((bf16[64,8,1024]{2,1,0:T(8,128)(2,1)}), bf16[64,8,1024]{2,1,0:T(8,128)(2,1)}, u32[]{:S(2)}, u32[]{:S(2)}) async-start(bf16[64,8,1024]{2,1,0:T(8,128)(2,1)} %stack.2), calls=%async_computation | async-start | bytes 2097152 | tf_op jit(solution)/shard_map/all_to_all | solution.py:58
  28.1 0.0 all-gather.2.cloned.1.call-start
  28.2 0.7 all-gather.2.cloned.1.call-update
  28.9 0.0 reduce-scatter.10.cloned.1.call-start
  30.2 0.2 copy.59
  30.5 0.2 copy.60
  30.7 0.9 copy.61
  31.7 0.5 compare_and_fusion.3
  32.2 0.6 broadcast_add_fusion
  32.8 0.9 bitcast_select_fusion.3
  33.7 141.4 %all-gather.2.cloned.1.call-done = bf16[512,1024]{1,0:T(8,128)(2,1)} async-done(((bf16[8,1024]{1,0:T(8,128)(2,1)}), bf16[512,1024]{1,0:T(8,128)(2,1)}) %all-gather.2.cloned.1.call-update) | async-done | bytes 1048592 | tf_op jit(solution)/shard_map/all_gather | solution.py:60
  175.1 1.5 copy.62
  176.6 0.7 copy.63
  177.2 1.9 gather_fusion.1
  179.2 2.3 convolution_bitcast_fusion
  181.5 3.5 copy.65
  185.0 3.8 convolution_bitcast_fusion.2
  188.8 0.2 copy.90
  189.0 1.0 copy.92
  190.0 0.0 reduce-scatter.10.cloned.1.call-update
  190.1 0.0 reduce-scatter.12.cloned.1.call-start
  190.1 0.1 compare_and_fusion
  190.2 0.0 all-to-all-done
  190.2 1.5 copy.96
  191.7 0.1 copy.67
  191.9 0.0 copy-start.1
  191.9 2.7 gather_fusion.2
  194.6 0.0 copy-done.1
  194.6 5.6 fusion.7
  200.2 6.6 %copy.68 = f32[512,24,128]{2,1,0:T(8,128)} copy(f32[512,24,128]{0,2,1:T(8,128)} %fusion.7) | data formatting | bytes 12582912 | tf_op jit(solution)/shard_map/rsk,skn->rsn/transpose | solution.py:14
  206.8 5.1 convolution_bitcast_fusion.1
  211.9 0.4 copy.91
  212.3 1.3 copy.94
  213.6 0.0 reduce-scatter.12.cloned.1.call-update
  213.6 0.0 reduce-scatter.8.cloned.1.call-start
  213.7 0.1 pad_add_fusion.1
  213.8 14.2 %reduce-scatter.10.cloned.1.call-done = f32[64,256]{1,0:T(8,128)} async-done(((f32[512,256]{1,0:T(8,128)}), f32[64,256]{1,0:T(8,128)}) %reduce-scatter.10.cloned.1.call-update) | async-done | bytes 65552 | tf_op jit(solution)/shard_map/reduce_scatter | solution.py:67
  228.0 49.8 %reduce-scatter.12.cloned.1.call-done = f32[64,512]{1,0:T(8,128)} async-done(((f32[512,512]{1,0:T(8,128)}), f32[64,512]{1,0:T(8,128)}) %reduce-scatter.12.cloned.1.call-update) | async-done | bytes 131088 | tf_op jit(solution)/shard_map/reduce_scatter | solution.py:61
  277.8 0.9 multiply_convert_fusion.2
  278.7 27.8 %all_gather.13 = bf16[512,256]{1,0:T(8,128)(2,1)S(1)} all-gather(bf16[64,256]{1,0:T(8,128)(2,1)S(1)} %get-tuple-element.31), channel_id=1, replica_groups=mesh['wide'=64,'narrow'=8] {'narrow'}, dimensions={0}, use_global_device_ids=true | all-gather | bytes 294912 | tf_op jit(solution)/shard_map/all_gather | solution.py:83
  306.5 0.1 copy.74
  306.7 28.6 %all_gather.14 = bf16[512,256]{1,0:T(8,128)(2,1)S(1)} all-gather(bf16[64,256]{1,0:T(8,128)(2,1)S(1)} %get-tuple-element.32), channel_id=1, replica_groups=mesh['wide'=64,'narrow'=8] {'narrow'}, dimensions={0}, use_global_device_ids=true | all-gather | bytes 294912 | tf_op jit(solution)/shard_map/all_gather | solution.py:84
  335.3 0.1 copy.75
  335.5 0.3 copy.76
  335.8 2.7 gather_fusion.3
  338.5 5.7 fusion.10
  344.1 6.6 %copy.78 = f32[512,24,128]{2,1,0:T(8,128)} copy(f32[512,24,128]{0,2,1:T(8,128)} %fusion.10) | data formatting | bytes 12582912 | tf_op jit(solution)/shard_map/rsn,skn->rsk/transpose | solution.py:14
  350.7 4.3 fusion.42
  355.0 0.0 copy-start.11
  355.0 1.8 copy.99
  356.8 0.0 reduce-scatter.8.cloned.1.call-update
  356.9 0.6 pad_add_fusion
  357.5 28.4 %all_gather.15 = bf16[512,256]{1,0:T(8,128)(2,1)S(1)} all-gather(bf16[64,256]{1,0:T(8,128)(2,1)S(1)} %get-tuple-element.33), channel_id=1, replica_groups=mesh['wide'=64,'narrow'=8] {'narrow'}, dimensions={0}, use_global_device_ids=true | all-gather | bytes 294912 | tf_op jit(solution)/shard_map/all_gather | solution.py:82
  385.9 0.1 copy.80
  386.0 0.2 copy.81
  386.2 1.9 gather_fusion
  388.2 2.8 fusion.33
  391.0 0.9 copy.84
  391.9 3.2 select_convert_fusion
  395.2 1.0 slice_bitcast_fusion
  396.1 179.4 %reduce-scatter.8.cloned.1.call-done = f32[8,1024]{1,0:T(8,128)} async-done(((f32[512,1024]{1,0:T(8,128)}), f32[8,1024]{1,0:T(8,128)}) %reduce-scatter.8.cloned.1.call-update) | async-done | bytes 32784 | tf_op jit(solution)/shard_map/reduce_scatter | solution.py:91
  575.6 1.4 convert_element_type.27
  (30 shorter events, 0.1 us)
Async XLA Ops:
  7.2 23.0 %copy-start.2 = (bf16[1,1,12,128,128]{4,3,2,1,0:T(8,128)(2,1)S(1)}, bf16[1,1,12,128,128]{4,3,2,1,0:T(8,128)(2,1)}, u32[]{:S(2)}) copy-start(bf16[1,1,12,128,128]{4,3,2,1,0:T(8,128)(2,1)} %param.17) | copy-start | bytes 1179652
  7.2 23.3 %copy-start.3 = (bf16[1,1,12,128,128]{4,3,2,1,0:T(8,128)(2,1)S(1)}, bf16[1,1,12,128,128]{4,3,2,1,0:T(8,128)(2,1)}, u32[]{:S(2)}) copy-start(bf16[1,1,12,128,128]{4,3,2,1,0:T(8,128)(2,1)} %param.18) | copy-start | bytes 1179652
  7.2 23.5 %copy-start.4 = (bf16[1,1,12,128,128]{4,3,2,1,0:T(8,128)(2,1)S(1)}, bf16[1,1,12,128,128]{4,3,2,1,0:T(8,128)(2,1)}, u32[]{:S(2)}) copy-start(bf16[1,1,12,128,128]{4,3,2,1,0:T(8,128)(2,1)} %param.21) | copy-start | bytes 1179652
  7.2 24.5 %copy-start.10 = (s32[1,1,12]{2,1,0:T(1,128)S(1)}, s32[1,1,12]{2,1,0:T(1,128)}, u32[]{:S(2)}) copy-start(s32[1,1,12]{2,1,0:T(1,128)} %param.22) | copy-start | bytes 148
  7.2 25.0 %copy-start.12 = (s32[1,1,12]{2,1,0:T(1,128)S(1)}, s32[1,1,12]{2,1,0:T(1,128)}, u32[]{:S(2)}) copy-start(s32[1,1,12]{2,1,0:T(1,128)} %param.19) | copy-start | bytes 148
  9.1 181.1 %all-to-all-start = ((bf16[64,8,1024]{2,1,0:T(8,128)(2,1)}), bf16[64,8,1024]{2,1,0:T(8,128)(2,1)}, u32[]{:S(2)}, u32[]{:S(2)}) async-start(bf16[64,8,1024]{2,1,0:T(8,128)(2,1)} %stack.2), calls=%async_computation | async-start | bytes 2097152 | tf_op jit(solution)/shard_map/all_to_all | solution.py:58
  28.1 146.9 %all-gather.2.cloned.1.call-start = ((), (), s32[]{:S(2)}) async-start(), calls=%async_computation.4 | async-start | bytes 1064960 | tf_op jit(solution)/shard_map/all_gather | solution.py:60
  28.9 199.1 %reduce-scatter.10.cloned.1.call-start = ((), (), s32[]{:S(2)}) async-start(), calls=%async_computation.6 | async-start | bytes 589824 | tf_op jit(solution)/shard_map/reduce_scatter | solution.py:67
  31.6 147.5 %copy-start.8 = (pred[12]{0:T(512)(128)(4,1)}, pred[12]{0:T(512)(128)(4,1)S(1)}, u32[]{:S(2)}) copy-start(pred[12]{0:T(512)(128)(4,1)S(1)} %iota_compare_fusion.3) | copy-start | bytes 40
  185.0 5.1 copy-start.5
  185.0 5.1 copy-start.6
  185.0 5.1 copy-start.7
  190.1 87.7 %reduce-scatter.12.cloned.1.call-start = ((), (), s32[]{:S(2)}) async-start(), calls=%async_computation.7 | async-start | bytes 1179648 | tf_op jit(solution)/shard_map/reduce_scatter | solution.py:61
  191.9 2.7 copy-start.1
  213.6 361.9 %reduce-scatter.8.cloned.1.call-start = ((), (), s32[]{:S(2)}) async-start(), calls=%async_computation.5 | async-start | bytes 2129920 | tf_op jit(solution)/shard_map/reduce_scatter | solution.py:91
  355.0 1.9 copy-start.9
  355.0 2.4 copy-start.11
  388.2 3.8 copy-start
Sparse Core Ops, SparseCore 0:
  32.2 142.7 all-gather.1
  190.2 37.7 reduce-scatter.9
  230.8 46.9 reduce-scatter.11
  357.0 218.5 reduce-scatter.7
